TPU v7x, 32 devices: a whole 2x2x4 slice. The times are simulated.
32 devices in a mesh: gx: 2 (over x), gz: 4 (over y, core), ta: 4 (over z).
Axes of the slice: x: 2, y: 2, z: 4, core: 2. Of those that a mesh axis runs over, the one named last changes fastest.
Arguments:
- velocity: bfloat16 [3, 32, 64, 4096], P(None, 'ta', 'gx', 'gz'), may hold values from -6 to 6
- offsets: int32 [7], replicated, may hold values from 0 to 16, as said below
- owner: int32 [7], replicated, may hold values from 0 to 7, as said below
Outputs:
- cross_spectra: float32 [4, 2, 7, 64, 4096], P(None, None, None, 'gx', ('gz', 'ta'))
Inputs may be any that keep to these rules, and one draw needn't show every extreme that they name: `offsets`: each segment of 16 snapshots lies inside the window. owner o names the block of streamwise index o // 4 and spanwise index o mod 4.
All inputs are finite; a program needn't handle non-finite values.
Results may differ from a plain program's by a relative error of at most 0.0062.
Values may be sent and summed in bfloat16 or wider, within the bound.
No kernel may reach another device: no remote copies, remote signals or barrier semaphores. Data moves between devices by JAX's collectives and lax.ppermute only.
A program may use at most 64 MiB of HBM per device.

v0:
```python
import math
import jax
import jax.numpy as jnp
from jax import lax
from jax.sharding import PartitionSpec as P

SEG = 16
NSEG = 7
F = 7


def from_root(shard, axis, root):
    mine = lax.axis_index(axis) == root
    return lax.psum(jnp.where(mine, shard, jnp.zeros_like(shard)), axis)


def padded_2(shard, sides, width):
    for axis, dim in sides:
        devices, length = (lax.axis_size(axis), shard.shape[dim])
        up = [(i, (i + 1) % devices) for i in range(devices)]
        down = [(j, i) for i, j in up]
        last = lax.slice_in_dim(shard, length - width, length, axis=dim)
        first = lax.slice_in_dim(shard, 0, width, axis=dim)
        before = lax.ppermute(last, axis, up)
        after = lax.ppermute(first, axis, down)
        shard = jnp.concatenate([before, shard, after], axis=dim)
    return shard


def dft_table(offsets, step_count_total):
    sample_times = jnp.arange(step_count_total, dtype=jnp.int32)
    temporal_delay = sample_times[None, :] - offsets[:, None]
    inside = (temporal_delay >= 0) & (temporal_delay < SEG)
    window = 0.5 - 0.5 * jnp.cos(2.0 * math.pi / SEG * temporal_delay.astype(jnp.float32))
    frequency = jnp.arange(1, F + 1, dtype=jnp.int32)
    turns = frequency[None, :, None] * temporal_delay[:, None, :] % SEG
    phase_angle = 2.0 * math.pi / SEG * turns.astype(jnp.float32)
    weight = jnp.where(inside, window, jnp.float32(0.0))[:, None, :]
    rows = jnp.stack([weight * jnp.cos(phase_angle), -weight * jnp.sin(phase_angle)], axis=1)
    return rows.reshape(offsets.shape[0] * 2 * F, step_count_total).astype(jnp.bfloat16)


def fourth_order(padded, which_axis, length_cells):

    def shifted(first):
        return lax.slice_in_dim(padded, first, first + length_cells, axis=which_axis)

    return (8.0 * (shifted(3) - shifted(1)) - (shifted(4) - shifted(0))) / 12.0


def spread_series(block_data, root_index):
    return from_root(block_data, ("gx", "gz"), root_index)


def shards(velocity, offsets, owner):
    block_rows = velocity.shape[2]
    block_cols = velocity.shape[3]
    stream_span = jnp.stack([velocity[0], velocity[2]])
    padded = padded_2(stream_span, (("gx", 2), ("gz", 3)), 2).astype(jnp.float32)
    streamwise = padded[0, :, 2 : 2 + block_rows, :]
    spanwise = padded[1, :, :, 2 : 2 + block_cols]
    vorticity = (
        fourth_order(streamwise, 2, block_cols) - fourth_order(spanwise, 1, block_rows)
    ).astype(jnp.bfloat16)
    fields = jnp.concatenate([velocity, vorticity[None]], axis=0)
    step_count_total = velocity.shape[1] * lax.axis_size("ta")
    segment_rows = dft_table(offsets, step_count_total)
    series = lax.all_to_all(fields, "ta", split_axis=3, concat_axis=1, tiled=True)
    flat_series = series.reshape(series.shape[0], series.shape[1], -1)
    power_spectra = jnp.einsum(
        "rt,qtn->qrn", segment_rows, flat_series, preferred_element_type=jnp.float32
    )
    flat_series, power_spectra = (flat_series, power_spectra)
    quantities = flat_series.shape[0]
    cells_here = flat_series.shape[2]
    slab_cols = cells_here // block_rows
    window_rows = dft_table(jnp.zeros((1,), jnp.int32), SEG)
    cospectrum = jnp.zeros((quantities, F, cells_here), jnp.float32)
    quadrature_spectrum = jnp.zeros((quantities, F, cells_here), jnp.float32)
    for segment in range(NSEG):
        local_spec = power_spectra[:, segment * 2 * F : (segment + 1) * 2 * F, :]
        window_piece = lax.dynamic_slice_in_dim(flat_series, offsets[segment], SEG, 1)
        arrived = spread_series(window_piece, owner[segment])
        remote = jnp.einsum("rt,qtn->qrn", window_rows, arrived, preferred_element_type=jnp.float32)
        remote_cos = remote[:, :F]
        remote_sin = remote[:, F:]
        cosine_part_here = local_spec[:, :F]
        local_sin = local_spec[:, F:]
        cospectrum = cospectrum + (remote_cos * cosine_part_here + remote_sin * local_sin)
        quadrature_spectrum = quadrature_spectrum + (
            remote_cos * local_sin - remote_sin * cosine_part_here
        )
    scaling = 8.0 / (3.0 * SEG * NSEG)
    result = jnp.stack([cospectrum, quadrature_spectrum], axis=1) * scaling
    return result.reshape(quantities, 2, F, block_rows, slab_cols)


def solution(mesh):
    in_specs = (P(None, "ta", "gx", "gz"), P(), P())
    out_specs = P(None, None, None, "gx", ("gz", "ta"))
    return jax.shard_map(shards, mesh=mesh, in_specs=in_specs, out_specs=out_specs, check_vma=False)
```

profile of v0, /device:TPU:0, one launch (start us, length us, event | category | flops | bytes accessed | tf_op | source)
XLA Modules:
  0.0 293.2 jit_solution(14867775583435725023)
XLA Ops:
  6.5 1.3 fusion.28
  8.1 3.0 %collective-permute-start = (bf16[2,8,2,1024]{3,1,2,0:T(8,128)(2,1)S(1)}, bf16[2,8,2,1024]{3,1,2,0:T(8,128)(2,1)S(1)}, u32[]{:S(2)}, u32[]{:S(2)}) collective-permute-start(bf16[2,8,2,1024]{3,1,2,0:T(8,128)(2,1)S(1)} %copy.47), channel_id=1, source_target_pairs={{0,16},{16,0},{1,17},{17,1},{2,18},{18,2},{3,19},{19,3},{4,20},{20... | collective-permute-start | bytes 196616 | tf_op jit(solution)/shard_map/ppermute | solution.py:24
  11.2 2.2 collective-permute-done
  14.0 1.5 collective-permute-done.1
  15.7 1.7 collective-permute-start.3
  17.4 6.1 %copy.34 = bf16[3,8,32,1024]{2,1,0,3:T(8,128)(2,1)} copy(bf16[3,8,32,1024]{3,2,1,0:T(8,128)(2,1)S(1)} %copy-done) | data formatting | bytes 3145728 | tf_op args[0]
  23.5 1.4 concatenate.11
  24.8 4.7 %copy.33 = bf16[2,8,36,1028]{2,1,3,0:T(8,128)(2,1)} copy(bf16[2,8,36,1028]{3,1,2,0:T(8,128)(2,1)S(1)} %concatenate.11) | data formatting | bytes 2368512 | tf_op jit(solution)/shard_map/concatenate | solution.py:26
  29.5 2.5 convert_element_type.78
  32.4 1.2 slice_bitcast_fusion
  33.6 4.4 %fusion.8 = bf16[1,8,32,1024]{2,1,0,3:T(8,128)(2,1)} fusion(f32[8,36,1024]{1,0,2:T(8,128)S(1)} %slice_bitcast_fusion.1, f32[8,32,1028]{1,0,2:T(8,128)S(1)} %slice_bitcast_fusion), kind=kLoop, calls=%fused_computation.23 | loop fusion | flops 3145728 | bytes 8912896 | tf_op jit(solution)/shard_map/broadcast_in_dim | solution.py:65
  38.1 6.7 %fusion.33 = bf16[1024,4,8,32]{3,2,1,0:T(8,128)(2,1)} fusion(bf16[1,8,32,1024]{2,1,0,3:T(8,128)(2,1)} %fusion.8, bf16[3,8,32,1024]{2,1,0,3:T(8,128)(2,1)S(1)} %bitcast.65), kind=kLoop, calls=%fused_computation.82 | loop fusion | flops 1048576 | bytes 4194304
  44.8 10.6 %reshape.340 = bf16[4,2,131072]{2,1,0:T(2,128)(2,1)} reshape(bf16[1024,4,8,32]{3,2,1,0:T(8,128)(2,1)} %fusion.33) | data formatting | bytes 4194304
  55.4 5.0 %all-to-all-start = ((bf16[4,2,131072]{2,1,0:T(2,128)(2,1)}), bf16[4,2,131072]{2,1,0:T(2,128)(2,1)S(1)}, u32[]{:S(2)}, u32[]{:S(2)}) async-start(bf16[4,2,131072]{2,1,0:T(2,128)(2,1)} %reshape.340), calls=%async_computation | async-start | bytes 4194304 | tf_op jit(solution)/shard_map/all_to_all | solution.py:68
  60.4 0.7 fusion.32
  69.8 0.7 fusion.31
  79.1 29.5 %all-to-all-done = bf16[4,2,131072]{2,1,0:T(2,128)(2,1)S(1)} async-done(((bf16[4,2,131072]{2,1,0:T(2,128)(2,1)}), bf16[4,2,131072]{2,1,0:T(2,128)(2,1)S(1)}, u32[]{:S(2)}, u32[]{:S(2)}) %all-to-all-start) | async-done | bytes 2097184 | tf_op jit(solution)/shard_map/all_to_all | solution.py:68
  108.6 5.6 %reshape.341 = bf16[1024,4,8,32]{3,2,1,0:T(8,128)(2,1)} reshape(bf16[4,2,131072]{2,1,0:T(2,128)(2,1)S(1)} %all-to-all-done) | data formatting | bytes 4194304
  114.3 8.8 %copy.35 = bf16[4,8,32,4,256]{4,1,2,3,0:T(8,128)(2,1)S(1)} copy(bf16[4,8,32,4,256]{2,1,0,4,3:T(8,128)(2,1)} %bitcast.63) | data formatting | bytes 4194304 | tf_op jit(solution)/shard_map/all_to_all | solution.py:68
  123.1 4.5 %dynamic-slice_select_fusion.6 = (bf16[4,16,8192]{2,1,0:T(8,128)(2,1)}, bf16[4,16,8192]{2,1,0:T(8,128)(2,1)}, bf16[4,16,8192]{2,1,0:T(8,128)(2,1)}, bf16[4,16,81...) fusion(bf16[4,32,8192]{2,1,0:T(8,128)(2,1)S(1)} %bitcast.61, ...), kind=kLoop, calls=%fused_computation.35 | loop fusion | flops 3670016 | bytes 14680099 | tf_op jit(solution)/shard_map/jit(_where)/select_n | solution.py:14
  128.3 7.6 %convolution_bitcast_fusion = f32[4,98,8192]{2,1,0:T(8,128)} fusion(bf16[4,32,8192]{2,1,0:T(8,128)(2,1)S(1)} %bitcast.62, bf16[98,32]{1,0:T(8,128)(2,1)S(1)} %convert_element_type.85), kind=kOutput, calls=%fused_computation | convolution fusion | flops 205520896 | bytes 14948480 | tf_op jit(solution)/shard_map/rt,qtn->qrn/dot_general | solution.py:70
  135.9 105.2 %all-reduce.3.cloned.1.call-done = (bf16[4,16,8192]{2,1,0:T(8,128)(2,1)}, bf16[4,16,8192]{2,1,0:T(8,128)(2,1)}, bf16[4,16,8192]{2,1,0:T(8,128)(2,1)}, bf16[4,16,...) async-done(((bf16[4,16,8192]{2,1,0:T(8,128)(2,1)}, bf16[4,16,8192]{2,1,0:T(8,128)(2,1)}, ...) | async-done | bytes 7340048 | tf_op jit(solution)/shard_map/psum | solution.py:14
  241.1 1.7 convolution_bitcast_fusion.1
  243.3 0.8 copy-done.6
  244.6 1.7 convolution_bitcast_fusion.4
  246.3 1.7 convolution_bitcast_fusion.5
  248.1 1.7 convolution_bitcast_fusion.6
  249.8 1.8 convolution_bitcast_fusion.7
  251.6 15.3 %subtract_add_fusion = f32[4,7,8192]{2,1,0:T(8,128)} fusion(f32[4,98,8192]{2,1,0:T(8,128)} %convolution_bitcast_fusion, f32[4,14,8192]{2,1,0:T(8,128)S(1)} %convolution_bitcast_fusion.1, f32[4,14,8192]{2,1,0:T(8,128)S(1)} %convolution_bitcast_fusion.2, f32[4,14,8192]{2,1,0:T(8,128)S(1)} %convolution_bitcast_fusion.3, ...), kind=kLoop, calls=%fused_computation.27 | loop fusion | flops 6193152 | bytes 26607616 | tf_op jit(solution)/shard_map/add | solution.py:90
  266.9 15.6 %add_add_fusion = f32[4,7,8192]{2,1,0:T(8,128)} fusion(f32[4,98,8192]{2,1,0:T(8,128)} %convolution_bitcast_fusion, f32[4,14,8192]{2,1,0:T(8,128)S(1)} %convolution_bitcast_fusion.1, f32[4,14,8192]{2,1,0:T(8,128)S(1)} %convolution_bitcast_fusion.2, f32[4,14,8192]{2,1,0:T(8,128)S(1)} %convolution_bitcast_fusion.3, ...), kind=kLoop, calls=%fused_computation.28 | loop fusion | flops 6193152 | bytes 26607616 | tf_op jit(solution)/shard_map/add | solution.py:89
  282.6 1.8 reshape.339
  285.1 1.3 copy.39
  (53 shorter events, 3.6 us)
Async XLA Ops:
  7.9 9.5 %copy-start = (bf16[3,8,32,1024]{3,2,1,0:T(8,128)(2,1)S(1)}, bf16[3,8,32,1024]{3,2,1,0:T(8,128)(2,1)}, u32[]{:S(2)}) copy-start(bf16[3,8,32,1024]{3,2,1,0:T(8,128)(2,1)} %param.3) | copy-start | bytes 4718596
  8.1 5.3 %collective-permute-start = (bf16[2,8,2,1024]{3,1,2,0:T(8,128)(2,1)S(1)}, bf16[2,8,2,1024]{3,1,2,0:T(8,128)(2,1)S(1)}, u32[]{:S(2)}, u32[]{:S(2)}) collective-permute-start(bf16[2,8,2,1024]{3,1,2,0:T(8,128)(2,1)S(1)} %copy.47), channel_id=1, source_target_pairs={{0,16},{16,0},{1,17},{17,1},{2,18},{18,2},{3,19},{19,3},{4,20},{20... | collective-permute-start | bytes 196616 | tf_op jit(solution)/shard_map/ppermute | solution.py:24
  11.1 4.3 %collective-permute-start.1 = (bf16[2,8,2,1024]{3,1,2,0:T(8,128)(2,1)S(1)}, bf16[2,8,2,1024]{3,1,2,0:T(8,128)(2,1)S(1)}, u32[]{:S(2)}, u32[]{:S(2)}) collective-permute-start(bf16[2,8,2,1024]{3,1,2,0:T(8,128)(2,1)S(1)} %copy.48), channel_id=1, source_target_pairs={{16,0},{0,16},{17,1},{1,17},{18,2},{2,18},{19,3},{3,19},{20,4},{4,... | collective-permute-start | bytes 196616 | tf_op jit(solution)/shard_map/ppermute | solution.py:25
  15.6 7.9 %collective-permute-start.2 = (bf16[2,8,36,2]{3,1,2,0:T(8,128)(2,1)S(1)}, bf16[2,8,36,2]{3,1,2,0:T(8,128)(2,1)S(1)}, u32[]{:S(2)}, u32[]{:S(2)}) collective-permute-start(bf16[2,8,36,2]{3,1,2,0:T(8,128)(2,1)S(1)} %get-tuple-element.22), channel_id=1, source_target_pairs={{0,4},{4,8},{8,12},{12,0},{1,5},{5,9},{9,13},{13,1},{2,6},{6,10},{... | collective-permute-start | bytes 6920 | tf_op jit(solution)/shard_map/ppermute | solution.py:24
  15.7 7.8 %collective-permute-start.3 = (bf16[2,8,36,2]{3,1,2,0:T(8,128)(2,1)S(1)}, bf16[2,8,36,2]{3,1,2,0:T(8,128)(2,1)S(1)}, u32[]{:S(2)}, u32[]{:S(2)}) collective-permute-start(bf16[2,8,36,2]{3,1,2,0:T(8,128)(2,1)S(1)} %get-tuple-element.21), channel_id=1, source_target_pairs={{4,0},{8,4},{12,8},{0,12},{5,1},{9,5},{13,9},{1,13},{6,2},{10,6},{... | collective-permute-start | bytes 6920 | tf_op jit(solution)/shard_map/ppermute | solution.py:25
  32.3 5.7 %slice-start = ((s8[6291456]{0:T(1024)(128)(4,1)}), s8[4194304]{0:T(1024)(128)(4,1)S(1)}, s32[]{:S(2)}) async-start(s8[6291456]{0:T(1024)(128)(4,1)} %bitcast.64), calls=%async_computation.2 | async-start | bytes 8388608
  33.6 4.5 %slice-start.1 = ((s8[6291456]{0:T(1024)(128)(4,1)}), s8[2097152]{0:T(1024)(128)(4,1)S(1)}, s32[]{:S(2)}) async-start(s8[6291456]{0:T(1024)(128)(4,1)} %bitcast.64), calls=%async_computation.3 | async-start | bytes 4194304
  55.4 5.0 %copy-start.8 = (s32[7]{0:T(128)S(1)}, s32[7]{0:T(128)}, u32[]{:S(2)}) copy-start(s32[7]{0:T(128)} %param.4) | copy-start | bytes 88
  55.4 14.4 %copy-start.9 = (s32[7]{0:T(128)S(1)}, s32[7]{0:T(128)}, u32[]{:S(2)}) copy-start(s32[7]{0:T(128)} %param.5) | copy-start | bytes 88
  55.4 53.3 %all-to-all-start = ((bf16[4,2,131072]{2,1,0:T(2,128)(2,1)}), bf16[4,2,131072]{2,1,0:T(2,128)(2,1)S(1)}, u32[]{:S(2)}, u32[]{:S(2)}) async-start(bf16[4,2,131072]{2,1,0:T(2,128)(2,1)} %reshape.340), calls=%async_computation | async-start | bytes 4194304 | tf_op jit(solution)/shard_map/all_to_all | solution.py:68
  60.4 180.7 %all-reduce.3.cloned.1.call-start = ((), (), s32[]{:S(2)}) async-start(), calls=%async_computation.1 | async-start | bytes 14680064 | tf_op jit(solution)/shard_map/psum | solution.py:14
  241.1 1.7 copy-start.7
  242.9 1.2 copy-start.6
  243.3 1.3 copy-start.5
  244.5 1.8 copy-start.4
  246.3 1.8 copy-start.3
  248.1 1.7 copy-start.2
  282.6 1.8 copy-start.1
Sparse Core Ops, SparseCore 0:
  127.8 113.3 all-reduce.2
where the time goes:
time: 294 us; the launch traced here: 293 us
  waiting for transfers between devices  138 us (47%)
  other arithmetic  50.1 us (17%)
  local copies, waits for them, and re-layouts  46.7 us (16%)
  between operations  31 us (11%)
  matrix products  17.1 us (6%)
  starting transfers between devices  9.91 us (3%)
    psum x1, waiting for transfers between devices, from_root(): return lax.psum(jnp.where(mine, shard, jnp.zeros_like(shard)), axis)  105 us
    all_to_all x1, waiting for transfers between devices, shards(): lax.all_to_all(fields, 'ta', split_axis=3, concat_axis=1, tiled=True)  29.5 us
    unnamed x31, local copies, waits for them, and re-layouts  23.8 us
    add x1, other arithmetic, shards(): cospectrum + (remote_cos * cosine_part_here + remote_sin * local_sin)  15.6 us
    add x1, other arithmetic, shards(): quadrature_spectrum + (remote_cos * local_sin - remote_sin * cosine_part_...  15.3 us
    dot_general x7, matrix products, shards(): jnp.einsum('rt,qtn->qrn', window_rows, arrived, preferred_element_type=jn...  9.5 us
    all_to_all x1, local copies, waits for them, and re-layouts, shards(): lax.all_to_all(fields, 'ta', split_axis=3, concat_axis=1, tiled=True)  8.82 us
    dot_general x1, matrix products, shards(): jnp.einsum('rt,qtn->qrn', segment_rows, flat_series, preferred_element_ty...  7.59 us
  transfers between devices with their start and end apart: 6, of which 4 were waited for; matrix products, arithmetic and copies ran while one was open for 6% of the time, Pallas kernels for 0%

commit v1 on v0

--- a/solution.py
+++ b/solution.py
@@ -65,7 +65,10 @@
     fields = jnp.concatenate([velocity, vorticity[None]], axis=0)
     step_count_total = velocity.shape[1] * lax.axis_size("ta")
     segment_rows = dft_table(offsets, step_count_total)
-    series = lax.all_to_all(fields, "ta", split_axis=3, concat_axis=1, tiled=True)
+    series = jnp.concatenate(
+        lax.all_to_all(jnp.stack(jnp.split(fields, lax.axis_size("ta"), axis=3)), "ta", 0, 0),
+        axis=1,
+    )
     flat_series = series.reshape(series.shape[0], series.shape[1], -1)
     power_spectra = jnp.einsum(
         "rt,qtn->qrn", segment_rows, flat_series, preferred_element_type=jnp.float32

time: 294 us -> 257 us (0.87)
  local copies, waits for them, and re-layouts: 46.7 us -> 14.1 us
  other arithmetic: 50.1 us -> 40 us
  waiting for transfers between devices: 138 us -> 144 us
    unnamed x31 -> x22, local copies, waits for them, and re-layouts: 23.8 us -> 2.76 us
    all_to_all x1 -> x0, local copies, waits for them, and re-layouts: 8.82 us -> none  [shards(): lax.all_to_all(fields, 'ta', split_axis=3, concat_axis=1, tiled=True)]
    unnamed x2 -> x0, other arithmetic: 6.74 us -> none
    concatenate x3 -> x1, local copies, waits for them, and re-layouts: 6.07 us -> 1.46 us  [padded_2(): shard = jnp.concatenate([before, shard, after], axis=dim)]
    broadcast_in_dim x1, other arithmetic: 4.44 us -> 0.88 us  [shards(): fields = jnp.concatenate([velocity, vorticity[None]], axis=0)]
    reshape x0 -> x1, local copies, waits for them, and re-layouts: none -> 3.01 us  [shards(): jnp.concatenate(lax.all_to_all(jnp.stack(jnp.split(fields, lax.axis_size(...]
    ppermute x2, starting transfers between devices: 3.09 us -> 0.14 us  [padded_2(): before = lax.ppermute(last, axis, up)]
    ppermute x2, starting transfers between devices: 1.82 us -> 4.76 us  [padded_2(): after = lax.ppermute(first, axis, down)]
  transfers between devices with their start and end apart: 6 -> 6, of which waited for: 4 -> 6; matrix products, arithmetic and copies ran while one was open for 6% -> 4% of each run, Pallas kernels for 0% -> 0%
where the time goes in v1:
time: 257 us
  waiting for transfers between devices  144 us (56%)
  other arithmetic  40 us (16%)
  between operations  31.7 us (12%)
  matrix products  17.3 us (7%)
  local copies, waits for them, and re-layouts  14.1 us (5%)
  starting transfers between devices  9.91 us (4%)
    psum x1, waiting for transfers between devices, from_root(): return lax.psum(jnp.where(mine, shard, jnp.zeros_like(shard)), axis)  106 us
    all_to_all x1, waiting for transfers between devices, shards(): lax.all_to_all(jnp.stack(jnp.split(fields, lax.axis_size('ta'), axis=3)),...  29.8 us
    add x1, other arithmetic, shards(): quadrature_spectrum + (remote_cos * local_sin - remote_sin * cosine_part_...  15.5 us
    add x1, other arithmetic, shards(): cospectrum + (remote_cos * cosine_part_here + remote_sin * local_sin)  15.3 us
    dot_general x7, matrix products, shards(): jnp.einsum('rt,qtn->qrn', window_rows, arrived, preferred_element_type=jn...  9.52 us
    dot_general x1, matrix products, shards(): jnp.einsum('rt,qtn->qrn', segment_rows, flat_series, preferred_element_ty...  7.8 us
  transfers between devices with their start and end apart: 6, of which 6 were waited for; matrix products, arithmetic and copies ran while one was open for 4% of the time, Pallas kernels for 0%

profile of v1, /device:TPU:0, one launch (start us, length us, event | category | flops | bytes accessed | tf_op | source)
XLA Modules:
  0.0 256.8 jit_solution(14168843192717132232)
XLA Ops:
  6.5 1.3 fusion.35
  7.9 3.0 %collective-permute-start.1 = (bf16[2,8,2,1024]{3,2,1,0:T(2,128)(2,1)S(1)}, bf16[2,8,2,1024]{3,2,1,0:T(2,128)(2,1)S(1)}, u32[]{:S(2)}, u32[]{:S(2)}) collective-permute-start(bf16[2,8,2,1024]{3,2,1,0:T(2,128)(2,1)S(1)} %get-tuple-element.28), channel_id=1, source_target_pairs={{16,0},{0,16},{17,1},{1,17},{18,2},{2,18},{19,3},{3,19},{20,4},{4,... | collective-permute-start | bytes 196616 | tf_op jit(solution)/shard_map/ppermute | solution.py:25
  11.1 2.3 collective-permute-done.1
  13.3 1.9 collective-permute-done
  15.2 0.7 pad_maximum_fusion.2
  16.2 1.7 collective-permute-start.3
  17.9 3.0 %collective-permute-done.2 = bf16[2,8,36,2]{3,2,1,0:T(8,128)(2,1)S(1)} collective-permute-done((bf16[2,8,36,2]{3,2,1,0:T(8,128)(2,1)S(1)}, bf16[2,8,36,2]{3,2,1,0:T(8,128)(2,1)S(1)}, u32[]{:S(2)}, u32[]{:S(2)}) %collective-permute-start.2) | collective-permute-done | bytes 2336 | tf_op jit(solution)/shard_map/ppermute | solution.py:24
  20.9 0.8 collective-permute-done.3
  21.7 1.5 concatenate.11
  23.9 0.9 fusion.15
  24.8 0.5 copy-done.1
  25.6 1.6 pad_maximum_fusion
  27.2 5.0 %all-to-all-start = ((bf16[4,4,8,32,256]{4,3,2,1,0:T(8,128)(2,1)}), bf16[4,4,8,32,256]{4,3,2,1,0:T(8,128)(2,1)S(1)}, u32[]{:S(2)}, u32[]{:S(2)}) async-start(bf16[4,4,8,32,256]{4,3,2,1,0:T(8,128)(2,1)} %pad_maximum_fusion), calls=%async_computation | async-start | bytes 4194304 | tf_op jit(solution)/shard_map/all_to_all | solution.py:69
  32.2 0.7 fusion.38
  41.9 0.7 fusion.37
  51.7 29.8 %all-to-all-done = bf16[4,4,8,32,256]{4,3,2,1,0:T(8,128)(2,1)S(1)} async-done(((bf16[4,4,8,32,256]{4,3,2,1,0:T(8,128)(2,1)}), bf16[4,4,8,32,256]{4,3,2,1,0:T(8,128)(2,1)S(1)}, u32[]{:S(2)}, u32[]{:S(2)}) %all-to-all-start) | async-done | bytes 2097184 | tf_op jit(solution)/shard_map/all_to_all | solution.py:69
  81.4 1.4 copy-done
  82.8 3.0 %copy.7 = bf16[4,4,8,32,256]{4,2,3,1,0:T(8,128)(2,1)S(1)} copy(bf16[4,4,8,32,256]{4,3,2,0,1:T(8,128)(2,1)} %bitcast.66) | data formatting | bytes 4194304 | tf_op jit(solution)/shard_map/reshape | solution.py:68
  85.8 4.5 %dynamic-slice_select_fusion.6 = (bf16[4,16,8192]{2,1,0:T(8,128)(2,1)}, bf16[4,16,8192]{2,1,0:T(8,128)(2,1)}, bf16[4,16,8192]{2,1,0:T(8,128)(2,1)}, bf16[4,16,81...) fusion(bf16[4,32,8192]{2,1,0:T(8,128)(2,1)S(1)} %bitcast.64, ...), kind=kLoop, calls=%fused_computation.40 | loop fusion | flops 3670016 | bytes 14680099 | tf_op jit(solution)/shard_map/jit(_where)/select_n | solution.py:14
  91.0 7.8 %convolution_bitcast_fusion = f32[4,98,8192]{2,1,0:T(8,128)} fusion(bf16[4,32,8192]{2,1,0:T(8,128)(2,1)S(1)} %bitcast.65, bf16[98,32]{1,0:T(8,128)(2,1)S(1)} %convert_element_type.85), kind=kOutput, calls=%fused_computation | convolution fusion | flops 205520896 | bytes 14948480 | tf_op jit(solution)/shard_map/rt,qtn->qrn/dot_general | solution.py:73
  98.8 106.0 %all-reduce.3.cloned.1.call-done = (bf16[4,16,8192]{2,1,0:T(8,128)(2,1)}, bf16[4,16,8192]{2,1,0:T(8,128)(2,1)}, bf16[4,16,8192]{2,1,0:T(8,128)(2,1)}, bf16[4,16,...) async-done(((bf16[4,16,8192]{2,1,0:T(8,128)(2,1)}, bf16[4,16,8192]{2,1,0:T(8,128)(2,1)}, ...) | async-done | bytes 7340048 | tf_op jit(solution)/shard_map/psum | solution.py:14
  204.8 1.7 convolution_bitcast_fusion.1
  207.0 0.8 copy-done.7
  208.3 1.8 convolution_bitcast_fusion.4
  210.0 1.7 convolution_bitcast_fusion.5
  211.8 1.7 convolution_bitcast_fusion.6
  213.5 1.8 convolution_bitcast_fusion.7
  215.2 15.5 %subtract_add_fusion = f32[4,7,8192]{2,1,0:T(8,128)} fusion(f32[4,98,8192]{2,1,0:T(8,128)} %convolution_bitcast_fusion, f32[4,14,8192]{2,1,0:T(8,128)S(1)} %convolution_bitcast_fusion.1, f32[4,14,8192]{2,1,0:T(8,128)S(1)} %convolution_bitcast_fusion.2, f32[4,14,8192]{2,1,0:T(8,128)S(1)} %convolution_bitcast_fusion.3, ...), kind=kLoop, calls=%fused_computation.32 | loop fusion | flops 6193152 | bytes 26607616 | tf_op jit(solution)/shard_map/add | solution.py:93
  230.8 15.3 %add_add_fusion = f32[4,7,8192]{2,1,0:T(8,128)} fusion(f32[4,98,8192]{2,1,0:T(8,128)} %convolution_bitcast_fusion, f32[4,14,8192]{2,1,0:T(8,128)S(1)} %convolution_bitcast_fusion.1, f32[4,14,8192]{2,1,0:T(8,128)S(1)} %convolution_bitcast_fusion.2, f32[4,14,8192]{2,1,0:T(8,128)S(1)} %convolution_bitcast_fusion.3, ...), kind=kLoop, calls=%fused_computation.33 | loop fusion | flops 6193152 | bytes 26607616 | tf_op jit(solution)/shard_map/add | solution.py:92
  246.1 1.8 reshape.338
  247.9 0.5 reshape.337
  248.6 1.3 copy.11
  (42 shorter events, 3.1 us)
Async XLA Ops:
  7.9 5.4 %collective-permute-start.1 = (bf16[2,8,2,1024]{3,2,1,0:T(2,128)(2,1)S(1)}, bf16[2,8,2,1024]{3,2,1,0:T(2,128)(2,1)S(1)}, u32[]{:S(2)}, u32[]{:S(2)}) collective-permute-start(bf16[2,8,2,1024]{3,2,1,0:T(2,128)(2,1)S(1)} %get-tuple-element.28), channel_id=1, source_target_pairs={{16,0},{0,16},{17,1},{1,17},{18,2},{2,18},{19,3},{3,19},{20,4},{4,... | collective-permute-start | bytes 196616 | tf_op jit(solution)/shard_map/ppermute | solution.py:25
  11.0 4.3 %collective-permute-start = (bf16[2,8,2,1024]{3,2,1,0:T(2,128)(2,1)S(1)}, bf16[2,8,2,1024]{3,2,1,0:T(2,128)(2,1)S(1)}, u32[]{:S(2)}, u32[]{:S(2)}) collective-permute-start(bf16[2,8,2,1024]{3,2,1,0:T(2,128)(2,1)S(1)} %get-tuple-element.27), channel_id=1, source_target_pairs={{0,16},{16,0},{1,17},{17,1},{2,18},{18,2},{3,19},{19,3},{4,20},{20... | collective-permute-start | bytes 196616 | tf_op jit(solution)/shard_map/ppermute | solution.py:24
  16.1 4.8 %collective-permute-start.2 = (bf16[2,8,36,2]{3,2,1,0:T(8,128)(2,1)S(1)}, bf16[2,8,36,2]{3,2,1,0:T(8,128)(2,1)S(1)}, u32[]{:S(2)}, u32[]{:S(2)}) collective-permute-start(bf16[2,8,36,2]{3,2,1,0:T(8,128)(2,1)S(1)} %get-tuple-element.26), channel_id=1, source_target_pairs={{0,4},{4,8},{8,12},{12,0},{1,5},{5,9},{9,13},{13,1},{2,6},{6,10},{... | collective-permute-start | bytes 6920 | tf_op jit(solution)/shard_map/ppermute | solution.py:24
  16.2 5.5 %collective-permute-start.3 = (bf16[2,8,36,2]{3,2,1,0:T(8,128)(2,1)S(1)}, bf16[2,8,36,2]{3,2,1,0:T(8,128)(2,1)S(1)}, u32[]{:S(2)}, u32[]{:S(2)}) collective-permute-start(bf16[2,8,36,2]{3,2,1,0:T(8,128)(2,1)S(1)} %get-tuple-element.25), channel_id=1, source_target_pairs={{4,0},{8,4},{12,8},{0,12},{5,1},{9,5},{13,9},{1,13},{6,2},{10,6},{... | collective-permute-start | bytes 6920 | tf_op jit(solution)/shard_map/ppermute | solution.py:25
  23.9 1.4 copy-start.1
  27.2 5.0 %copy-start.9 = (s32[7]{0:T(128)S(1)}, s32[7]{0:T(128)}, u32[]{:S(2)}) copy-start(s32[7]{0:T(128)} %param.4) | copy-start | bytes 88
  27.2 14.7 %copy-start.10 = (s32[7]{0:T(128)S(1)}, s32[7]{0:T(128)}, u32[]{:S(2)}) copy-start(s32[7]{0:T(128)} %param.5) | copy-start | bytes 88
  27.2 54.2 %all-to-all-start = ((bf16[4,4,8,32,256]{4,3,2,1,0:T(8,128)(2,1)}), bf16[4,4,8,32,256]{4,3,2,1,0:T(8,128)(2,1)S(1)}, u32[]{:S(2)}, u32[]{:S(2)}) async-start(bf16[4,4,8,32,256]{4,3,2,1,0:T(8,128)(2,1)} %pad_maximum_fusion), calls=%async_computation | async-start | bytes 4194304 | tf_op jit(solution)/shard_map/all_to_all | solution.py:69
  32.2 172.6 %all-reduce.3.cloned.1.call-start = ((), (), s32[]{:S(2)}) async-start(), calls=%async_computation.1 | async-start | bytes 14680064 | tf_op jit(solution)/shard_map/psum | solution.py:14
  81.4 1.4 copy-start
  204.8 1.7 copy-start.8
  206.5 1.2 copy-start.7
  206.9 1.3 copy-start.6
  208.2 1.9 copy-start.5
  210.0 1.7 copy-start.4
  211.8 1.7 copy-start.3
  246.1 1.8 copy-start.2
Sparse Core Ops, SparseCore 0:
  90.4 114.2 all-reduce.2
